TPU v7x, 256 devices: a whole 4x4x8 slice. The times are simulated.
256 devices in a mesh: seq: 16 (over z_lo, y), head: 16 (over x, z_hi, core).
Axes of the slice: x: 4, y: 4, z: 8 (z_hi: 2, z_lo: 4; z = z_hi * 4 + z_lo), core: 2. Of those that a mesh axis runs over, the one named last changes fastest.
Arguments:
- query: bfloat16 [16384, 2048], P(('seq', 'head')), may hold values from -6 to 6
- key: bfloat16 [16384, 2048], P(('seq', 'head')), may hold values from -6 to 6
- value: bfloat16 [16384, 2048], P(('seq', 'head')), may hold values from -6 to 6
- output: bfloat16 [16384, 2048], P(('seq', 'head')), may hold values from -6 to 6
- grad_out: bfloat16 [16384, 2048], P(('seq', 'head')), may hold values from -6 to 6
- logsumexp: float32 [16, 16384], P('head', 'seq'), may hold values from 3.5 to 8.5, as said below
- rand_blocks: int32 [256, 3], replicated, may hold values from 0 to 255, as said below
Outputs:
- grad_query: bfloat16 [16384, 2048], P(('seq', 'head'))
- grad_key: bfloat16 [16384, 2048], P(('seq', 'head'))
- grad_value: bfloat16 [16384, 2048], P(('seq', 'head'))
Inputs may be any that keep to these rules, and one draw needn't show every extreme that they name: `rand_blocks`: each row names 3 different blocks, none below 2 and none within one block of the row's own block. In aligned runs of 16 rows, exactly 3 of the run's entries fall in each aligned run of 16 key blocks. `logsumexp`: rows of the first 2 blocks lie between 7 and 8.5, all others between 3.5 and 5.
All inputs are finite; a program needn't handle non-finite values.
Results may differ from a plain program's by a relative error of at most 0.02.
Values may be sent and summed in bfloat16 or wider, within the bound.
No kernel may reach another device: no remote copies, remote signals or barrier semaphores. Data moves between devices by JAX's collectives and lax.ppermute only.
A program may use at most 64 MiB of HBM per device.

v0:
```python
import jax
import jax.numpy as jnp
from jax import lax
from jax.sharding import PartitionSpec as P

HEADS = 16
HD = 128
BLK = 64
GLOB = 2
RAND = 3


def spread(value, axis, source):
    kept = jnp.where(lax.axis_index(axis) == source, value, 0).astype(value.dtype)
    return lax.psum(kept, axis)


def passed_along(value, axis, steps):
    count = lax.axis_size(axis)
    initial, last = (max(0, -steps), min(count, count - steps))
    return lax.ppermute(value, axis, [(source, source + steps) for source in range(initial, last)])


def block_grads(queries, grad_rows, log_norm, deltas, keys, values, usable, factor):
    scores = (
        jnp.einsum("...md,...nd->...mn", queries, keys, preferred_element_type=jnp.float32) * factor
    )
    weights = jnp.where(usable, jnp.exp(scores - log_norm[..., None]), 0.0)
    weights_low = weights.astype(jnp.bfloat16)
    grad_values = jnp.einsum(
        "...mn,...md->...nd", weights_low, grad_rows, preferred_element_type=jnp.float32
    )
    grad_probs = jnp.einsum(
        "...md,...nd->...mn", grad_rows, values, preferred_element_type=jnp.float32
    )
    grad_scores = (weights * (grad_probs - deltas[..., None])).astype(jnp.bfloat16)
    grad_queries = (
        jnp.einsum("...mn,...nd->...md", grad_scores, keys, preferred_element_type=jnp.float32)
        * factor
    )
    grad_keys = (
        jnp.einsum("...mn,...md->...nd", grad_scores, queries, preferred_element_type=jnp.float32)
        * factor
    )
    return (grad_queries, grad_keys, grad_values)


def slide_blocks(stack, offset):
    if offset == 0:
        return stack
    blank = jnp.zeros_like(stack[:, :1])
    if offset > 0:
        return jnp.concatenate([stack[:, 1:], blank], axis=1)
    return jnp.concatenate([blank, stack[:, :-1]], axis=1)


def slot_order(rand_blocks, group_id, blocks_here):
    pattern_rows = lax.dynamic_slice_in_dim(rand_blocks, group_id * blocks_here, blocks_here, 0)
    entries = pattern_rows.reshape(-1)
    ranking = jnp.argsort(entries // blocks_here, stable=True)
    slot_query = ranking // rand_blocks.shape[1]
    slot_key = entries[ranking] % blocks_here
    return (slot_query, slot_key)


def per_device(query, key, value, output, grad_out, logsumexp, rand_blocks):
    tok_rows = query.shape[0]
    heads_here = logsumexp.shape[0]
    seq_rows = logsumexp.shape[1]
    blocks_here = seq_rows // BLK
    groups = lax.axis_size("seq")
    position = lax.axis_index("seq")
    per_group = RAND * blocks_here // groups
    glob_rows = GLOB * BLK
    factor = HD ** (-0.5)

    def to_heads(matrix):
        return matrix.reshape(tok_rows, HEADS, HD).transpose(1, 0, 2)

    query_rows, key_rows, value_rows, out_rows, grad_rows = (
        lax.all_to_all(to_heads(query), "head", split_axis=0, concat_axis=1, tiled=True),
        lax.all_to_all(to_heads(key), "head", split_axis=0, concat_axis=1, tiled=True),
        lax.all_to_all(to_heads(value), "head", split_axis=0, concat_axis=1, tiled=True),
        lax.all_to_all(to_heads(output), "head", split_axis=0, concat_axis=1, tiled=True),
        lax.all_to_all(to_heads(grad_out), "head", split_axis=0, concat_axis=1, tiled=True),
    )
    deltas = jnp.sum(grad_rows.astype(jnp.float32) * out_rows.astype(jnp.float32), axis=-1)

    def as_blocks(stack):
        return stack.reshape((heads_here, blocks_here, BLK) + stack.shape[2:])

    query_blk = as_blocks(query_rows)
    key_blk = as_blocks(key_rows)
    value_blk = as_blocks(value_rows)
    grad_blk = as_blocks(grad_rows)
    norm_blk = as_blocks(logsumexp)
    delta_blk = as_blocks(deltas)
    block_ids = jnp.arange(blocks_here, dtype=jnp.int32)
    first_id = position * blocks_here
    query_alive = first_id + block_ids >= GLOB
    grad_query = jnp.zeros((heads_here, blocks_here, BLK, HD), jnp.float32)
    grad_key_home = jnp.zeros_like(grad_query)
    grad_value_home = jnp.zeros_like(grad_query)
    for offset in (-1, 0, 1):
        target = block_ids + offset
        usable = query_alive & (target >= 0) & (target < blocks_here) & (first_id + target >= GLOB)
        part_q, part_k, part_v = block_grads(
            query_blk,
            grad_blk,
            norm_blk,
            delta_blk,
            slide_blocks(key_blk, offset),
            slide_blocks(value_blk, offset),
            usable[None, :, None, None],
            factor,
        )
        grad_query = grad_query + part_q
        grad_key_home = grad_key_home + slide_blocks(part_k, -offset)
        grad_value_home = grad_value_home + slide_blocks(part_v, -offset)
    row_alive = jnp.repeat(query_alive, BLK)
    at_home = (position == 0).astype(jnp.float32)
    glob_key, glob_value, glob_query, glob_grad = (
        spread(key_rows[:, :glob_rows], "seq", 0),
        spread(value_rows[:, :glob_rows], "seq", 0),
        spread(query_rows[:, :glob_rows], "seq", 0),
        spread(grad_rows[:, :glob_rows], "seq", 0),
    )
    glob_norm, glob_delta = (
        spread(logsumexp[:, :glob_rows], "seq", 0),
        spread(deltas[:, :glob_rows], "seq", 0),
    )
    key_part_q, key_part_k, key_part_v = block_grads(
        query_rows,
        grad_rows,
        logsumexp,
        deltas,
        glob_key,
        glob_value,
        row_alive[None, :, None],
        factor,
    )
    grad_query = grad_query + as_blocks(key_part_q)
    spread_q, spread_k, spread_v = block_grads(
        glob_query, glob_grad, glob_norm, glob_delta, key_rows, value_rows, True, factor
    )
    grad_key_home = grad_key_home + as_blocks(spread_k)
    grad_value_home = grad_value_home + as_blocks(spread_v)
    totals_k, totals_v, totals_q = (
        lax.psum(key_part_k.astype(jnp.bfloat16), "seq").astype(jnp.float32),
        lax.psum(key_part_v.astype(jnp.bfloat16), "seq").astype(jnp.float32),
        lax.psum(spread_q.astype(jnp.bfloat16), "seq").astype(jnp.float32),
    )
    grad_query = grad_query.at[:, :GLOB].add(at_home * totals_q.reshape(heads_here, GLOB, BLK, HD))
    grad_key_home = grad_key_home.at[:, :GLOB].add(
        at_home * totals_k.reshape(heads_here, GLOB, BLK, HD)
    )
    grad_value_home = grad_value_home.at[:, :GLOB].add(
        at_home * totals_v.reshape(heads_here, GLOB, BLK, HD)
    )
    slot_q = slot_order(rand_blocks, position, blocks_here)[0]

    def wanted(anchor):
        return slot_order(rand_blocks, anchor, blocks_here)[1]

    all_wanted = jax.vmap(wanted)(jnp.arange(groups, dtype=jnp.int32))
    send_ids = lax.dynamic_slice_in_dim(all_wanted, position * per_group, per_group, 1).reshape(-1)
    far_key, far_value = (
        lax.all_to_all(key_blk[:, send_ids], "seq", split_axis=1, concat_axis=1, tiled=True),
        lax.all_to_all(value_blk[:, send_ids], "seq", split_axis=1, concat_axis=1, tiled=True),
    )
    usable = first_id + slot_q >= GLOB
    part_q, part_k, part_v = block_grads(
        query_blk[:, slot_q],
        grad_blk[:, slot_q],
        norm_blk[:, slot_q],
        delta_blk[:, slot_q],
        far_key,
        far_value,
        usable[None, :, None, None],
        factor,
    )
    grad_query = grad_query.at[:, slot_q].add(part_q)
    back_key, back_value = (
        lax.all_to_all(part_k, "seq", split_axis=1, concat_axis=1, tiled=True),
        lax.all_to_all(part_v, "seq", split_axis=1, concat_axis=1, tiled=True),
    )
    grad_key_home = grad_key_home.at[:, send_ids].add(back_key)
    grad_value_home = grad_value_home.at[:, send_ids].add(back_value)
    left_key, left_value = passed_along((key_blk[:, -1:], value_blk[:, -1:]), "seq", 1)
    right_key, right_value = passed_along((key_blk[:, :1], value_blk[:, :1]), "seq", -1)
    left_ok = (position >= 1) & (first_id - 1 >= GLOB)
    right_ok = (position <= groups - 2) & (first_id + blocks_here - 1 >= GLOB)
    left_q, left_k, left_v = block_grads(
        query_blk[:, :1],
        grad_blk[:, :1],
        norm_blk[:, :1],
        delta_blk[:, :1],
        left_key,
        left_value,
        left_ok,
        factor,
    )
    right_q, right_k, right_v = block_grads(
        query_blk[:, -1:],
        grad_blk[:, -1:],
        norm_blk[:, -1:],
        delta_blk[:, -1:],
        right_key,
        right_value,
        right_ok,
        factor,
    )
    grad_query = grad_query.at[:, :1].add(left_q)
    grad_query = grad_query.at[:, -1:].add(right_q)
    from_right_k, from_right_v = (
        passed_along(left_k.astype(jnp.bfloat16), "seq", -1).astype(left_k.dtype),
        passed_along(left_v.astype(jnp.bfloat16), "seq", -1).astype(left_v.dtype),
    )
    from_left_k, from_left_v = (
        passed_along(right_k.astype(jnp.bfloat16), "seq", 1).astype(right_k.dtype),
        passed_along(right_v.astype(jnp.bfloat16), "seq", 1).astype(right_v.dtype),
    )
    grad_key_home = grad_key_home.at[:, -1:].add(from_right_k)
    grad_value_home = grad_value_home.at[:, -1:].add(from_right_v)
    grad_key_home = grad_key_home.at[:, :1].add(from_left_k)
    grad_value_home = grad_value_home.at[:, :1].add(from_left_v)

    def to_rows(stack):
        return stack.astype(jnp.bfloat16).reshape(heads_here, seq_rows, HD)

    back_q, back_k, back_v = (
        lax.all_to_all(to_rows(grad_query), "head", split_axis=1, concat_axis=0, tiled=True),
        lax.all_to_all(to_rows(grad_key_home), "head", split_axis=1, concat_axis=0, tiled=True),
        lax.all_to_all(to_rows(grad_value_home), "head", split_axis=1, concat_axis=0, tiled=True),
    )

    def to_tokens(stack):
        return stack.transpose(1, 0, 2).reshape(tok_rows, HEADS * HD)

    return (to_tokens(back_q), to_tokens(back_k), to_tokens(back_v))


def solution(mesh):
    in_specs = (
        P(("seq", "head"), None),
        P(("seq", "head"), None),
        P(("seq", "head"), None),
        P(("seq", "head"), None),
        P(("seq", "head"), None),
        P("head", "seq"),
        P(),
    )
    out_specs = (P(("seq", "head"), None), P(("seq", "head"), None), P(("seq", "head"), None))
    return jax.shard_map(
        per_device, mesh=mesh, in_specs=in_specs, out_specs=out_specs, check_vma=False
    )
```

profile of v0, /device:TPU:64, one launch (start us, length us, event | category | flops | bytes accessed | tf_op | source)
XLA Modules:
  0.0 658.4 jit_solution(3117383005306899725)
XLA Ops:
  8.9 9.2 %all-to-all-start = ((bf16[16,64,128]{2,1,0:T(8,128)(2,1)}), bf16[16,64,128]{2,1,0:T(8,128)(2,1)S(1)}, u32[]{:S(2)}, u32[]{:S(2)}) async-start(bf16[16,64,128]{2,1,0:T(8,128)(2,1)} %bitcast_bitcast_fusion.4), calls=%async_computation | async-start | bytes 524288 | tf_op jit(solution)/shard_map/all_to_all | solution.py:82
  18.2 32.0 %while.10 = (s32[]{:T(128)}, s32[256,3]{0,1:T(4,128)}, s32[16,2]{0,1:T(2,128)S(1)}, s32[16,16,3]{1,2,0:T(4,128)S(1)}, s32[]{:T(128)}) while((s32[]{:T(128)}, s32[256,3]{0,1:T(4,128)}, s32[16,2]{0,1:T(2,128)S(1)}, s32[16,16,3]{1,2,0:T(4,128)S(1)}, s32[]{:T(128)}) %tuple.65), condition=%wide.while_cond.9, body=%wide.while_body.9.sunk | while | flops 2 | bytes 2345 | solution.py:58
  51.5 5.3 gather_fusion.6
  57.4 2.0 sort.34
  61.6 9.6 %all-to-all-start.2 = ((bf16[16,64,128]{2,1,0:T(8,128)(2,1)}), bf16[16,64,128]{2,1,0:T(8,128)(2,1)S(1)}, u32[]{:S(2)}, u32[]{:S(2)}) async-start(bf16[16,64,128]{2,1,0:T(8,128)(2,1)} %bitcast_bitcast_fusion.2), calls=%async_computation.2 | async-start | bytes 524288 | tf_op jit(solution)/shard_map/all_to_all | solution.py:83
  72.1 13.9 %all-to-all-done.2 = bf16[16,64,128]{2,1,0:T(8,128)(2,1)S(1)} async-done(((bf16[16,64,128]{2,1,0:T(8,128)(2,1)}), bf16[16,64,128]{2,1,0:T(8,128)(2,1)S(1)}, u32[]{:S(2)}, u32[]{:S(2)}) %all-to-all-start.2) | async-done | bytes 262176 | tf_op jit(solution)/shard_map/all_to_all | solution.py:83
  86.0 3.5 all-to-all-start.4
  91.6 10.8 %all-to-all-done.4 = bf16[16,64,128]{2,1,0:T(8,128)(2,1)S(1)} async-done(((bf16[16,64,128]{2,1,0:T(8,128)(2,1)}), bf16[16,64,128]{2,1,0:T(8,128)(2,1)S(1)}, u32[]{:S(2)}, u32[]{:S(2)}) %all-to-all-start.4) | async-done | bytes 262176 | tf_op jit(solution)/shard_map/all_to_all | solution.py:84
  102.4 3.5 all-to-all-start.3
  109.1 8.8 %all-to-all-done.3 = bf16[16,64,128]{2,1,0:T(8,128)(2,1)S(1)} async-done(((bf16[16,64,128]{2,1,0:T(8,128)(2,1)}), bf16[16,64,128]{2,1,0:T(8,128)(2,1)S(1)}, u32[]{:S(2)}, u32[]{:S(2)}) %all-to-all-start.3) | async-done | bytes 262176 | tf_op jit(solution)/shard_map/all_to_all | solution.py:85
  118.0 3.5 all-to-all-start.1
  124.0 9.5 %all-to-all-done.1 = bf16[16,64,128]{2,1,0:T(8,128)(2,1)S(1)} async-done(((bf16[16,64,128]{2,1,0:T(8,128)(2,1)}), bf16[16,64,128]{2,1,0:T(8,128)(2,1)S(1)}, u32[]{:S(2)}, u32[]{:S(2)}) %all-to-all-start.1) | async-done | bytes 262176 | tf_op jit(solution)/shard_map/all_to_all | solution.py:81
  134.7 5.4 collective-permute-start.2
  140.1 1.9 collective-permute-start
  142.6 6.0 collective-permute-start.3
  148.7 1.9 collective-permute-start.1
  154.0 1.6 gather_fusion.1
  155.6 7.3 %all-to-all-start.5 = ((bf16[1,48,64,128]{3,2,0,1:T(8,128)(2,1)}), bf16[1,48,64,128]{3,2,0,1:T(8,128)(2,1)S(1)}, u32[]{:S(2)}, u32[]{:S(2)}) async-start(bf16[1,48,64,128]{3,2,0,1:T(8,128)(2,1)} %bitcast.32), calls=%async_computation.5 | async-start | bytes 1572864 | tf_op jit(solution)/shard_map/all_to_all | solution.py:168
  167.3 1.6 gather_fusion
  170.5 36.8 %all-reduce.9 = (f32[128]{0:T(128)}, f32[128]{0:T(128)S(1)}) all-reduce(f32[128]{0:T(128)S(1)} %copy-done.53, f32[128]{0:T(128)S(1)} %copy-done.54), channel_id=1, replica_groups=mesh['seq'=16,'head'=16] {'seq'}, use_global_device_ids=true, to_apply=%region_4.5 | all-reduce | flops 256 | bytes 2048 | tf_op jit(solution)/shard_map/psum | solution.py:15
  207.8 107.8 %all-reduce.17.cloned.1.call-done = (bf16[128,128]{1,0:T(8,128)(2,1)}, bf16[128,128]{1,0:T(8,128)(2,1)}, bf16[128,128]{1,0:T(8,128)(2,1)}, bf16[128,128]{1,0:T(8,128)(2,1)}) async-done(((bf16[128,128]{1,0:T(8,128)(2,1)}, bf16[128,128]{1,0:T(8,128)(2,1)}, bf16[128,128]{1,0:T(8,128)(2,1)}, bf16[128,128]{1,0:T(8,128)(2,1)}), (bf16[128,128]{1,0:T(8,128)(2,1)}, bf16[128,128]{1,0:T(8,128)(2,1)}, ...) | async-done | bytes 131088 | tf_op jit(solution)/shard_map/psum | solution.py:15
  320.6 14.9 %all-to-all-start.6 = ((bf16[1,48,64,128]{3,2,0,1:T(8,128)(2,1)}), bf16[1,48,64,128]{3,2,0,1:T(8,128)(2,1)}, u32[]{:S(2)}, u32[]{:S(2)}) async-start(bf16[1,48,64,128]{3,2,0,1:T(8,128)(2,1)} %bitcast.35), calls=%async_computation.6 | async-start | bytes 1572864 | tf_op jit(solution)/shard_map/all_to_all | solution.py:169
  340.1 144.8 %all-reduce.15.cloned.1.call-done = (bf16[1,128,128]{2,1,0:T(8,128)(2,1)}, bf16[1,128,128]{2,1,0:T(8,128)(2,1)}, bf16[1,128,128]{2,1,0:T(8,128)(2,1)}) async-done(((bf16[1,128,128]{2,1,0:T(8,128)(2,1)}, bf16[1,128,128]{2,1,0:T(8,128)(2,1)}, bf16[1,128,128]{2,1,0:T(8,128)(2,1)}), (bf16[1,128,128]{2,1,0:T(8,128)(2,1)}, bf16[1,128,128]{2,1,0:T(8,128)(2,1)}, ...) | async-done | bytes 98320 | tf_op jit(solution)/shard_map/psum | solution.py:151
  485.7 2.9 exponential_select_fusion
  488.6 2.3 multiply_convert_fusion
  492.5 5.4 scatter_fusion
  499.1 2.1 reduce.25
  502.0 8.2 %all-to-all-start.7 = ((bf16[16,2,4096]{2,1,0:T(2,128)(2,1)}), bf16[16,2,4096]{2,1,0:T(2,128)(2,1)S(1)}, u32[]{:S(2)}, u32[]{:S(2)}) async-start(bf16[16,2,4096]{2,1,0:T(2,128)(2,1)} %reshape.1100), calls=%async_computation.7 | async-start | bytes 524288 | tf_op jit(solution)/shard_map/all_to_all | solution.py:232
  510.3 3.0 convolution_bitcast_fusion
  513.3 9.0 %all-to-all-done.7 = bf16[16,2,4096]{2,1,0:T(2,128)(2,1)S(1)} async-done(((bf16[16,2,4096]{2,1,0:T(2,128)(2,1)}), bf16[16,2,4096]{2,1,0:T(2,128)(2,1)S(1)}, u32[]{:S(2)}, u32[]{:S(2)}) %all-to-all-start.7) | async-done | bytes 262176 | tf_op jit(solution)/shard_map/all_to_all | solution.py:232
  522.3 11.6 %all-to-all-start.10 = ((f32[1,48,64,128]{3,2,0,1:T(8,128)}), f32[1,48,64,128]{3,2,0,1:T(8,128)}, u32[]{:S(2)}, u32[]{:S(2)}) async-start(f32[1,48,64,128]{3,2,0,1:T(8,128)} %convolution_bitcast_fusion), calls=%async_computation.10 | async-start | bytes 3145728 | tf_op jit(solution)/shard_map/all_to_all | solution.py:185
  533.9 1.6 multiply_bitcast_fusion
  535.5 35.5 %all-to-all-done.10 = f32[1,48,64,128]{3,2,0,1:T(8,128)} async-done(((f32[1,48,64,128]{3,2,0,1:T(8,128)}), f32[1,48,64,128]{3,2,0,1:T(8,128)}, u32[]{:S(2)}, u32[]{:S(2)}) %all-to-all-start.10) | async-done | bytes 1572896 | tf_op jit(solution)/shard_map/all_to_all | solution.py:185
  571.0 5.1 all-to-all-start.8
  578.9 3.5 collective-permute-start.5
  582.6 4.6 collective-permute-start.4
  588.0 2.5 collective-permute-start.6
  591.2 3.4 collective-permute-start.7
  600.6 5.4 scatter_fusion.2
  606.0 3.5 collective-permute-done.6
  610.2 2.5 collective-permute-done.7
  613.9 2.1 reduce.27
  616.8 4.2 all-to-all-start.11
  621.8 2.9 scatter_fusion.1
  626.0 2.1 reduce.26
  628.9 4.0 all-to-all-done.11
  632.9 5.6 all-to-all-start.9
  640.7 9.8 %all-to-all-done.9 = bf16[16,2,4096]{2,1,0:T(2,128)(2,1)S(1)} async-done(((bf16[16,2,4096]{2,1,0:T(2,128)(2,1)}), bf16[16,2,4096]{2,1,0:T(2,128)(2,1)S(1)}, u32[]{:S(2)}, u32[]{:S(2)}) %all-to-all-start.9) | async-done | bytes 262176 | tf_op jit(solution)/shard_map/all_to_all | solution.py:233
  (309 shorter events, 90.4 us)
Async XLA Ops:
  8.9 52.7 %all-to-all-start = ((bf16[16,64,128]{2,1,0:T(8,128)(2,1)}), bf16[16,64,128]{2,1,0:T(8,128)(2,1)S(1)}, u32[]{:S(2)}, u32[]{:S(2)}) async-start(bf16[16,64,128]{2,1,0:T(8,128)(2,1)} %bitcast_bitcast_fusion.4), calls=%async_computation | async-start | bytes 524288 | tf_op jit(solution)/shard_map/all_to_all | solution.py:82
  51.5 8.8 %copy-start.39 = (f32[1,1024]{1,0:T(1,128)S(1)}, f32[1,1024]{1,0:T(1,128)}, u32[]{:S(2)}) copy-start(f32[1,1024]{1,0:T(1,128)} %param.30) | copy-start | bytes 12292
  51.5 9.3 %copy-start.27 = (bf16[64,2048]{1,0:T(8,128)(2,1)S(1)}, bf16[64,2048]{1,0:T(8,128)(2,1)}, u32[]{:S(2)}) copy-start(bf16[64,2048]{1,0:T(8,128)(2,1)} %param.27) | copy-start | bytes 786436
  51.5 19.8 %copy-start.28 = (bf16[64,2048]{1,0:T(8,128)(2,1)S(1)}, bf16[64,2048]{1,0:T(8,128)(2,1)}, u32[]{:S(2)}) copy-start(bf16[64,2048]{1,0:T(8,128)(2,1)} %param.28) | copy-start | bytes 786436
  56.8 33.2 %copy-start.29 = (bf16[64,2048]{1,0:T(8,128)(2,1)S(1)}, bf16[64,2048]{1,0:T(8,128)(2,1)}, u32[]{:S(2)}) copy-start(bf16[64,2048]{1,0:T(8,128)(2,1)} %param.25) | copy-start | bytes 786436
  56.9 34.0 %copy-start.30 = (bf16[64,2048]{1,0:T(8,128)(2,1)S(1)}, bf16[64,2048]{1,0:T(8,128)(2,1)}, u32[]{:S(2)}) copy-start(bf16[64,2048]{1,0:T(8,128)(2,1)} %param.29) | copy-start | bytes 786436
  60.0 31.6 %copy-start.49 = (s32[48]{0:T(128)}, s32[48]{0:T(128)S(1)}, u32[]{:S(2)}) copy-start(s32[48]{0:T(128)S(1)} %compare_select_fusion.3) | copy-start | bytes 580
  60.2 11.0 %copy-start.46 = (s32[48]{0:T(128)}, s32[48]{0:T(128)S(1)}, u32[]{:S(2)}) copy-start(s32[48]{0:T(128)S(1)} %fusion.115) | copy-start | bytes 580
  61.6 24.4 %all-to-all-start.2 = ((bf16[16,64,128]{2,1,0:T(8,128)(2,1)}), bf16[16,64,128]{2,1,0:T(8,128)(2,1)S(1)}, u32[]{:S(2)}, u32[]{:S(2)}) async-start(bf16[16,64,128]{2,1,0:T(8,128)(2,1)} %bitcast_bitcast_fusion.2), calls=%async_computation.2 | async-start | bytes 524288 | tf_op jit(solution)/shard_map/all_to_all | solution.py:83
  86.0 16.4 %all-to-all-start.4 = ((bf16[16,64,128]{2,1,0:T(8,128)(2,1)}), bf16[16,64,128]{2,1,0:T(8,128)(2,1)S(1)}, u32[]{:S(2)}, u32[]{:S(2)}) async-start(bf16[16,64,128]{2,1,0:T(8,128)(2,1)} %bitcast_bitcast_fusion), calls=%async_computation.4 | async-start | bytes 524288 | tf_op jit(solution)/shard_map/all_to_all | solution.py:84
  102.4 15.6 %all-to-all-start.3 = ((bf16[16,64,128]{2,1,0:T(8,128)(2,1)}), bf16[16,64,128]{2,1,0:T(8,128)(2,1)S(1)}, u32[]{:S(2)}, u32[]{:S(2)}) async-start(bf16[16,64,128]{2,1,0:T(8,128)(2,1)} %bitcast_bitcast_fusion.1), calls=%async_computation.3 | async-start | bytes 524288 | tf_op jit(solution)/shard_map/all_to_all | solution.py:85
  118.0 15.5 %all-to-all-start.1 = ((bf16[16,64,128]{2,1,0:T(8,128)(2,1)}), bf16[16,64,128]{2,1,0:T(8,128)(2,1)S(1)}, u32[]{:S(2)}, u32[]{:S(2)}) async-start(bf16[16,64,128]{2,1,0:T(8,128)(2,1)} %bitcast_bitcast_fusion.3), calls=%async_computation.1 | async-start | bytes 524288 | tf_op jit(solution)/shard_map/all_to_all | solution.py:81
  134.7 72.6 %collective-permute-start.2 = (bf16[1,1,64,128]{3,2,1,0:T(8,128)(2,1)S(1)}, bf16[1,1,64,128]{3,2,1,0:T(8,128)(2,1)S(1)}, u32[]{:S(2)}, u32[]{:S(2)}) collective-permute-start(bf16[1,1,64,128]{3,2,1,0:T(8,128)(2,1)S(1)} %get-tuple-element.144), channel_id=1, source_target_pairs={{16,0},{32,16},{48,32},{64,48},{80,64},{96,80},{112,96},{128,112},... | collective-permute-start | bytes 49160 | tf_op jit(solution)/shard_map/ppermute | solution.py:21
  140.1 67.4 %collective-permute-start = (bf16[1,1,64,128]{3,2,1,0:T(8,128)(2,1)S(1)}, bf16[1,1,64,128]{3,2,1,0:T(8,128)(2,1)S(1)}, u32[]{:S(2)}, u32[]{:S(2)}) collective-permute-start(bf16[1,1,64,128]{3,2,1,0:T(8,128)(2,1)S(1)} %get-tuple-element.145), channel_id=1, source_target_pairs={{0,16},{16,32},{32,48},{48,64},{64,80},{80,96},{96,112},{112,128},... | collective-permute-start | bytes 49160 | tf_op jit(solution)/shard_map/ppermute | solution.py:21
  142.6 64.8 %collective-permute-start.3 = (bf16[1,1,64,128]{3,2,1,0:T(8,128)(2,1)S(1)}, bf16[1,1,64,128]{3,2,1,0:T(8,128)(2,1)S(1)}, u32[]{:S(2)}, u32[]{:S(2)}) collective-permute-start(bf16[1,1,64,128]{3,2,1,0:T(8,128)(2,1)S(1)} %get-tuple-element.142), channel_id=1, source_target_pairs={{16,0},{32,16},{48,32},{64,48},{80,64},{96,80},{112,96},{128,112},... | collective-permute-start | bytes 49160 | tf_op jit(solution)/shard_map/ppermute | solution.py:21
  148.7 59.1 %collective-permute-start.1 = (bf16[1,1,64,128]{3,2,1,0:T(8,128)(2,1)S(1)}, bf16[1,1,64,128]{3,2,1,0:T(8,128)(2,1)S(1)}, u32[]{:S(2)}, u32[]{:S(2)}) collective-permute-start(bf16[1,1,64,128]{3,2,1,0:T(8,128)(2,1)S(1)} %get-tuple-element.143), channel_id=1, source_target_pairs={{0,16},{16,32},{32,48},{48,64},{64,80},{80,96},{96,112},{112,128},... | collective-permute-start | bytes 49160 | tf_op jit(solution)/shard_map/ppermute | solution.py:21
  154.0 9.7 %copy-start.55 = (pred[16]{0:T(512)(128)(4,1)S(1)}, pred[16]{0:T(512)(128)(4,1)}, u32[]{:S(2)}) copy-start(pred[16]{0:T(512)(128)(4,1)} %and_and_fusion) | copy-start | bytes 52
  155.6 165.0 %all-to-all-start.5 = ((bf16[1,48,64,128]{3,2,0,1:T(8,128)(2,1)}), bf16[1,48,64,128]{3,2,0,1:T(8,128)(2,1)S(1)}, u32[]{:S(2)}, u32[]{:S(2)}) async-start(bf16[1,48,64,128]{3,2,0,1:T(8,128)(2,1)} %bitcast.32), calls=%async_computation.5 | async-start | bytes 1572864 | tf_op jit(solution)/shard_map/all_to_all | solution.py:168
  163.0 152.7 %all-reduce.17.cloned.1.call-start = ((), (), s32[]{:S(2)}) async-start(), calls=%async_computation.13 | async-start | bytes 262144 | tf_op jit(solution)/shard_map/psum | solution.py:15
  168.9 146.7 %copy-start.48 = (pred[1024]{0:T(1024)(128)(4,1)S(1)}, pred[1024]{0:T(1024)(128)(4,1)}, u32[]{:S(2)}) copy-start(pred[1024]{0:T(1024)(128)(4,1)} %broadcast_in_dim.110) | copy-start | bytes 3076
  207.4 108.2 %copy-start.34 = (f32[64,64]{1,0:T(8,128)}, f32[64,64]{1,0:T(8,128)S(1)}, u32[]{:S(2)}) copy-start(f32[64,64]{1,0:T(8,128)S(1)} %fusion.41) | copy-start | bytes 49156
  207.5 111.3 %copy-start.44 = (bf16[1,1,64,128]{3,2,1,0:T(8,128)(2,1)}, bf16[1,1,64,128]{3,2,1,0:T(8,128)(2,1)S(1)}, u32[]{:S(2)}) copy-start(bf16[1,1,64,128]{3,2,1,0:T(8,128)(2,1)S(1)} %collective-permute-done) | copy-start | bytes 49156
  207.7 107.9 %copy-start.36 = (f32[64,64]{1,0:T(8,128)}, f32[64,64]{1,0:T(8,128)S(1)}, u32[]{:S(2)}) copy-start(f32[64,64]{1,0:T(8,128)S(1)} %fusion.46) | copy-start | bytes 49156
  320.6 15.1 %copy-start.10 = (bf16[128,1024]{1,0:T(8,128)(2,1)S(1)}, bf16[128,1024]{1,0:T(8,128)(2,1)}, u32[]{:S(2)}) copy-start(bf16[128,1024]{1,0:T(8,128)(2,1)} %fusion.30) | copy-start | bytes 786436
  320.6 16.8 %copy-start.33 = (bf16[128,128]{1,0:T(8,128)(2,1)S(1)}, bf16[128,128]{1,0:T(8,128)(2,1)}, u32[]{:S(2)}) copy-start(bf16[128,128]{1,0:T(8,128)(2,1)} %get-tuple-element.136) | copy-start | bytes 98308
  320.6 16.8 %copy-start.5 = (bf16[1,48,64,128]{3,2,0,1:T(8,128)(2,1)}, bf16[1,48,64,128]{3,2,0,1:T(8,128)(2,1)S(1)}, u32[]{:S(2)}) copy-start(bf16[1,48,64,128]{3,2,0,1:T(8,128)(2,1)S(1)} %all-to-all-done.5) | copy-start | bytes 2359300
  320.6 168.0 %all-to-all-start.6 = ((bf16[1,48,64,128]{3,2,0,1:T(8,128)(2,1)}), bf16[1,48,64,128]{3,2,0,1:T(8,128)(2,1)}, u32[]{:S(2)}, u32[]{:S(2)}) async-start(bf16[1,48,64,128]{3,2,0,1:T(8,128)(2,1)} %bitcast.35), calls=%async_computation.6 | async-start | bytes 1572864 | tf_op jit(solution)/shard_map/all_to_all | solution.py:169
  335.5 149.4 %all-reduce.15.cloned.1.call-start = ((), (), s32[]{:S(2)}) async-start(), calls=%async_computation.12 | async-start | bytes 196608 | tf_op jit(solution)/shard_map/psum | solution.py:151
  337.4 148.3 %copy-start.3 = (bf16[48,64,128]{2,1,0:T(8,128)(2,1)S(1)}, bf16[48,64,128]{2,1,0:T(8,128)(2,1)}, u32[]{:S(2)}) copy-start(bf16[48,64,128]{2,1,0:T(8,128)(2,1)} %gather_fusion) | copy-start | bytes 2359300
  337.5 148.3 %copy-start.51 = (pred[48]{0:T(512)(128)(4,1)S(1)}, pred[48]{0:T(512)(128)(4,1)}, u32[]{:S(2)}) copy-start(pred[48]{0:T(512)(128)(4,1)} %get-tuple-element.140) | copy-start | bytes 148
  338.7 147.0 %copy-start.43 = (f32[48,64]{1,0:T(8,128)S(1)}, f32[48,64]{1,0:T(8,128)}, u32[]{:S(2)}) copy-start(f32[48,64]{1,0:T(8,128)} %gather_fusion.2) | copy-start | bytes 36868
  502.0 20.3 %all-to-all-start.7 = ((bf16[16,2,4096]{2,1,0:T(2,128)(2,1)}), bf16[16,2,4096]{2,1,0:T(2,128)(2,1)S(1)}, u32[]{:S(2)}, u32[]{:S(2)}) async-start(bf16[16,2,4096]{2,1,0:T(2,128)(2,1)} %reshape.1100), calls=%async_computation.7 | async-start | bytes 524288 | tf_op jit(solution)/shard_map/all_to_all | solution.py:232
  513.3 20.6 %copy-start.4 = (bf16[48,64,128]{2,1,0:T(8,128)(2,1)S(1)}, bf16[48,64,128]{2,1,0:T(8,128)(2,1)}, u32[]{:S(2)}) copy-start(bf16[48,64,128]{2,1,0:T(8,128)(2,1)} %gather_fusion) | copy-start | bytes 2359300
  522.3 48.7 %all-to-all-start.10 = ((f32[1,48,64,128]{3,2,0,1:T(8,128)}), f32[1,48,64,128]{3,2,0,1:T(8,128)}, u32[]{:S(2)}, u32[]{:S(2)}) async-start(f32[1,48,64,128]{3,2,0,1:T(8,128)} %convolution_bitcast_fusion), calls=%async_computation.10 | async-start | bytes 3145728 | tf_op jit(solution)/shard_map/all_to_all | solution.py:185
  535.5 40.6 %copy-start.20 = (f32[16,64,64]{2,1,0:T(8,128)S(1)}, f32[16,64,64]{2,1,0:T(8,128)}, u32[]{:S(2)}) copy-start(f32[16,64,64]{2,1,0:T(8,128)} %copy-done.19) | copy-start | bytes 786436
  571.0 45.8 %all-to-all-start.8 = ((f32[1,48,64,128]{3,2,0,1:T(8,128)}), f32[1,48,64,128]{3,2,0,1:T(8,128)S(1)}, u32[]{:S(2)}, u32[]{:S(2)}) async-start(f32[1,48,64,128]{3,2,0,1:T(8,128)} %multiply_bitcast_fusion), calls=%async_computation.8 | async-start | bytes 3145728 | tf_op jit(solution)/shard_map/all_to_all | solution.py:184
  578.4 9.5 %copy-start.23 = (f32[1,16,64,128]{3,2,1,0:T(8,128)}, f32[1,16,64,128]{3,2,1,0:T(8,128)S(1)}, u32[]{:S(2)}) copy-start(f32[1,16,64,128]{3,2,1,0:T(8,128)S(1)} %fusion.2) | copy-start | bytes 1572868
  578.5 8.7 %copy-start.37 = (f32[64,64]{1,0:T(8,128)S(1)}, f32[64,64]{1,0:T(8,128)}, u32[]{:S(2)}) copy-start(f32[64,64]{1,0:T(8,128)} %copy-done.36) | copy-start | bytes 49156
  578.5 12.0 %copy-start.35 = (f32[64,64]{1,0:T(8,128)S(1)}, f32[64,64]{1,0:T(8,128)}, u32[]{:S(2)}) copy-start(f32[64,64]{1,0:T(8,128)} %copy-done.34) | copy-start | bytes 49156
  578.5 16.1 %copy-start.2 = (f32[128,1024]{1,0:T(8,128)S(1)}, f32[128,1024]{1,0:T(8,128)}, u32[]{:S(2)}) copy-start(f32[128,1024]{1,0:T(8,128)} %copy-done.1) | copy-start | bytes 1572868
  578.7 11.7 %copy-start.24 = (f32[1,16,64,128]{3,2,1,0:T(8,128)}, f32[1,16,64,128]{3,2,1,0:T(8,128)S(1)}, u32[]{:S(2)}) copy-start(f32[1,16,64,128]{3,2,1,0:T(8,128)S(1)} %fusion) | copy-start | bytes 1572868
  578.7 18.0 %copy-start.22 = (f32[16,64,64]{2,1,0:T(8,128)S(1)}, f32[16,64,64]{2,1,0:T(8,128)}, u32[]{:S(2)}) copy-start(f32[16,64,64]{2,1,0:T(8,128)} %copy-done.21) | copy-start | bytes 786436
  578.9 46.6 %collective-permute-start.5 = (bf16[1,1,64,128]{3,2,1,0:T(8,128)(2,1)S(1)}, bf16[1,1,64,128]{3,2,1,0:T(8,128)(2,1)S(1)}, u32[]{:S(2)}, u32[]{:S(2)}) collective-permute-start(bf16[1,1,64,128]{3,2,1,0:T(8,128)(2,1)S(1)} %fusion.58), channel_id=1, source_target_pairs={{0,16},{16,32},{32,48},{48,64},{64,80},{80,96},{96,112},{112,128},... | collective-permute-start | bytes 49160 | tf_op jit(solution)/shard_map/ppermute | solution.py:21
  582.6 42.2 %collective-permute-start.4 = (bf16[1,1,64,128]{3,2,1,0:T(8,128)(2,1)S(1)}, bf16[1,1,64,128]{3,2,1,0:T(8,128)(2,1)}, u32[]{:S(2)}, u32[]{:S(2)}) collective-permute-start(bf16[1,1,64,128]{3,2,1,0:T(8,128)(2,1)S(1)} %fusion.59), channel_id=1, source_target_pairs={{16,0},{32,16},{48,32},{64,48},{80,64},{96,80},{112,96},{128,112},... | collective-permute-start | bytes 49160 | tf_op jit(solution)/shard_map/ppermute | solution.py:21
  588.0 21.5 %collective-permute-start.6 = (bf16[1,1,64,128]{3,2,1,0:T(8,128)(2,1)}, bf16[1,1,64,128]{3,2,1,0:T(8,128)(2,1)}, u32[]{:S(2)}, u32[]{:S(2)}) collective-permute-start(bf16[1,1,64,128]{3,2,1,0:T(8,128)(2,1)} %fusion.56), channel_id=1, source_target_pairs={{16,0},{32,16},{48,32},{64,48},{80,64},{96,80},{112,96},{128,112},... | collective-permute-start | bytes 49160 | tf_op jit(solution)/shard_map/ppermute | solution.py:21
  591.2 21.5 %collective-permute-start.7 = (bf16[1,1,64,128]{3,2,1,0:T(8,128)(2,1)}, bf16[1,1,64,128]{3,2,1,0:T(8,128)(2,1)}, u32[]{:S(2)}, u32[]{:S(2)}) collective-permute-start(bf16[1,1,64,128]{3,2,1,0:T(8,128)(2,1)} %fusion.57), channel_id=1, source_target_pairs={{0,16},{16,32},{32,48},{48,64},{64,80},{80,96},{96,112},{112,128},... | collective-permute-start | bytes 49160 | tf_op jit(solution)/shard_map/ppermute | solution.py:21
  616.8 16.1 %all-to-all-start.11 = ((bf16[16,2,4096]{2,1,0:T(2,128)(2,1)}), bf16[16,2,4096]{2,1,0:T(2,128)(2,1)S(1)}, u32[]{:S(2)}, u32[]{:S(2)}) async-start(bf16[16,2,4096]{2,1,0:T(2,128)(2,1)} %reshape.1104), calls=%async_computation.11 | async-start | bytes 524288 | tf_op jit(solution)/shard_map/all_to_all | solution.py:234
  632.9 17.5 %all-to-all-start.9 = ((bf16[16,2,4096]{2,1,0:T(2,128)(2,1)}), bf16[16,2,4096]{2,1,0:T(2,128)(2,1)S(1)}, u32[]{:S(2)}, u32[]{:S(2)}) async-start(bf16[16,2,4096]{2,1,0:T(2,128)(2,1)} %reshape.1102), calls=%async_computation.9 | async-start | bytes 524288 | tf_op jit(solution)/shard_map/all_to_all | solution.py:233
  (32 other events, 62.1 us)
Sparse Core Ops, SparseCore 0:
  167.2 148.3 all-reduce.16
  339.4 145.4 all-reduce.14
where the time goes:
time: 661 us; the launch traced here: 658 us
  waiting for transfers between devices  361 us (55%)
  starting transfers between devices  116 us (18%)
  local copies, waits for them, and re-layouts  67.5 us (10%)
  blocking collectives  36.8 us (6%)
  other arithmetic  33.5 us (5%)
  matrix products  28.9 us (4%)
  between operations  15.3 us (2%)
    psum x1, waiting for transfers between devices, per_device(): lax.psum(spread_q.astype(jnp.bfloat16), 'seq').astype(jnp.float32)  145 us
    psum x1, waiting for transfers between devices, spread(): return lax.psum(kept, axis)  108 us
    psum x1, blocking collectives, spread(): return lax.psum(kept, axis)  36.8 us
    all_to_all x1, waiting for transfers between devices, per_device(): lax.all_to_all(part_v, 'seq', split_axis=1, concat_axis=1, tiled=True)  35.5 us
    gather x48, local copies, waits for them, and re-layouts  32 us
    ppermute x8, starting transfers between devices, passed_along(): lax.ppermute(value, axis, [(source, source + steps) for source in range(i...  29.1 us
    all_to_all x1, starting transfers between devices, per_device(): lax.all_to_all(value_blk[:, send_ids], 'seq', split_axis=1, concat_axis=1...  14.9 us
    all_to_all x1, waiting for transfers between devices, per_device(): lax.all_to_all(to_heads(value), 'head', split_axis=0, concat_axis=1, tile...  13.9 us
  transfers between devices with their start and end apart: 22, of which 12 were waited for; matrix products, arithmetic and copies ran while one was open for 16% of the time, Pallas kernels for 0%

commit v1 on v0

--- a/solution.py
+++ b/solution.py
@@ -228,9 +228,12 @@
     def to_rows(stack):
         return stack.astype(jnp.bfloat16).reshape(heads_here, seq_rows, HD)
 
+    watch_the_blocks = lambda mat: jnp.concatenate(
+        lax.all_to_all(jnp.stack(jnp.split(mat, lax.axis_size("head"), 1), 0), "head", 0, 0), 0
+    )
     back_q, back_k, back_v = (
         lax.all_to_all(to_rows(grad_query), "head", split_axis=1, concat_axis=0, tiled=True),
-        lax.all_to_all(to_rows(grad_key_home), "head", split_axis=1, concat_axis=0, tiled=True),
+        watch_the_blocks(to_rows(grad_key_home)),
         lax.all_to_all(to_rows(grad_value_home), "head", split_axis=1, concat_axis=0, tiled=True),
     )
 

time: 661 us -> 609 us (0.921)
  waiting for transfers between devices: 361 us -> 292 us
  local copies, waits for them, and re-layouts: 67.5 us -> 77.5 us
    all_to_all x1, waiting for transfers between devices: 35.5 us -> 4.7 us  [per_device(): lax.all_to_all(part_v, 'seq', split_axis=1, concat_axis=1, tiled=True)]
    psum x1, waiting for transfers between devices: 108 us -> 83 us  [spread(): return lax.psum(kept, axis)]
    all_to_all x1, starting transfers between devices: 5.1 us -> 14.7 us  [per_device(): lax.all_to_all(part_k, 'seq', split_axis=1, concat_axis=1, tiled=True)]
    unnamed x125 -> x133, local copies, waits for them, and re-layouts: 9.19 us -> 17.2 us
    all_to_all x1, waiting for transfers between devices: 9.02 us -> 1.19 us  [per_device(): lax.all_to_all(to_rows(grad_query), 'head', split_axis=1, concat_axis=0,...]
    all_to_all x1, waiting for transfers between devices: 4.05 us -> 11.4 us  [per_device(): lax.all_to_all(to_rows(grad_value_home), 'head', split_axis=1, concat_axi...]
  transfers between devices with their start and end apart: 22 -> 22, of which waited for: 12 -> 10; matrix products, arithmetic and copies ran while one was open for 16% -> 22% of each run, Pallas kernels for 0% -> 0%
where the time goes in v1:
time: 609 us; the launch traced here: 604 us
  waiting for transfers between devices  292 us (48%)
  starting transfers between devices  121 us (20%)
  local copies, waits for them, and re-layouts  77.5 us (13%)
  other arithmetic  36.8 us (6%)
  blocking collectives  34.8 us (6%)
  matrix products  27.1 us (4%)
  between operations  15.2 us (2%)
    psum x1, waiting for transfers between devices, per_device(): lax.psum(spread_q.astype(jnp.bfloat16), 'seq').astype(jnp.float32)  140 us
    psum x1, waiting for transfers between devices, spread(): return lax.psum(kept, axis)  83 us
    psum x1, blocking collectives, spread(): return lax.psum(kept, axis)  34.8 us
    gather x48, local copies, waits for them, and re-layouts  32 us
    ppermute x8, starting transfers between devices, passed_along(): lax.ppermute(value, axis, [(source, source + steps) for source in range(i...  29 us
    unnamed x133, local copies, waits for them, and re-layouts  17.2 us
    all_to_all x1, starting transfers between devices, per_device(): lax.all_to_all(part_k, 'seq', split_axis=1, concat_axis=1, tiled=True)  14.7 us
    all_to_all x1, waiting for transfers between devices, per_device(): lax.all_to_all(to_heads(value), 'head', split_axis=0, concat_axis=1, tile...  12.8 us
  transfers between devices with their start and end apart: 22, of which 10 were waited for; matrix products, arithmetic and copies ran while one was open for 22% of the time, Pallas kernels for 0%

profile of v1, /device:TPU:64, one launch (start us, length us, event | category | flops | bytes accessed | tf_op | source)
XLA Modules:
  0.0 604.3 jit_solution(11631536498174579379)
XLA Ops:
  8.9 9.2 %all-to-all-start = ((bf16[16,64,128]{2,1,0:T(8,128)(2,1)}), bf16[16,64,128]{2,1,0:T(8,128)(2,1)S(1)}, u32[]{:S(2)}, u32[]{:S(2)}) async-start(bf16[16,64,128]{2,1,0:T(8,128)(2,1)} %bitcast_bitcast_fusion.4), calls=%async_computation | async-start | bytes 524288 | tf_op jit(solution)/shard_map/all_to_all | solution.py:82
  18.2 32.0 %while.10 = (s32[]{:T(128)}, s32[256,3]{0,1:T(4,128)}, s32[16,2]{0,1:T(2,128)S(1)}, s32[16,16,3]{1,2,0:T(4,128)S(1)}, s32[]{:T(128)}) while((s32[]{:T(128)}, s32[256,3]{0,1:T(4,128)}, s32[16,2]{0,1:T(2,128)S(1)}, s32[16,16,3]{1,2,0:T(4,128)S(1)}, s32[]{:T(128)}) %tuple.65), condition=%wide.while_cond.9, body=%wide.while_body.9.sunk | while | flops 2 | bytes 2345 | solution.py:58
  51.5 5.3 gather_fusion.6
  57.4 2.0 sort.34
  62.6 9.6 %all-to-all-start.2 = ((bf16[16,64,128]{2,1,0:T(8,128)(2,1)}), bf16[16,64,128]{2,1,0:T(8,128)(2,1)S(1)}, u32[]{:S(2)}, u32[]{:S(2)}) async-start(bf16[16,64,128]{2,1,0:T(8,128)(2,1)} %bitcast_bitcast_fusion.2), calls=%async_computation.2 | async-start | bytes 524288 | tf_op jit(solution)/shard_map/all_to_all | solution.py:83
  74.2 12.8 %all-to-all-done.2 = bf16[16,64,128]{2,1,0:T(8,128)(2,1)S(1)} async-done(((bf16[16,64,128]{2,1,0:T(8,128)(2,1)}), bf16[16,64,128]{2,1,0:T(8,128)(2,1)S(1)}, u32[]{:S(2)}, u32[]{:S(2)}) %all-to-all-start.2) | async-done | bytes 262176 | tf_op jit(solution)/shard_map/all_to_all | solution.py:83
  87.0 3.5 all-to-all-start.4
  92.7 10.8 %all-to-all-done.4 = bf16[16,64,128]{2,1,0:T(8,128)(2,1)S(1)} async-done(((bf16[16,64,128]{2,1,0:T(8,128)(2,1)}), bf16[16,64,128]{2,1,0:T(8,128)(2,1)S(1)}, u32[]{:S(2)}, u32[]{:S(2)}) %all-to-all-start.4) | async-done | bytes 262176 | tf_op jit(solution)/shard_map/all_to_all | solution.py:84
  103.4 3.5 all-to-all-start.3
  110.7 8.3 %all-to-all-done.3 = bf16[16,64,128]{2,1,0:T(8,128)(2,1)S(1)} async-done(((bf16[16,64,128]{2,1,0:T(8,128)(2,1)}), bf16[16,64,128]{2,1,0:T(8,128)(2,1)S(1)}, u32[]{:S(2)}, u32[]{:S(2)}) %all-to-all-start.3) | async-done | bytes 262176 | tf_op jit(solution)/shard_map/all_to_all | solution.py:85
  119.0 3.5 all-to-all-start.1
  125.1 9.4 %all-to-all-done.1 = bf16[16,64,128]{2,1,0:T(8,128)(2,1)S(1)} async-done(((bf16[16,64,128]{2,1,0:T(8,128)(2,1)}), bf16[16,64,128]{2,1,0:T(8,128)(2,1)S(1)}, u32[]{:S(2)}, u32[]{:S(2)}) %all-to-all-start.1) | async-done | bytes 262176 | tf_op jit(solution)/shard_map/all_to_all | solution.py:81
  135.7 5.4 collective-permute-start.2
  141.1 1.9 collective-permute-start
  143.7 6.0 collective-permute-start.3
  149.7 1.9 collective-permute-start.1
  154.1 1.7 gather_fusion.1
  155.8 7.3 %all-to-all-start.5 = ((bf16[1,48,64,128]{3,2,0,1:T(8,128)(2,1)}), bf16[1,48,64,128]{3,2,0,1:T(8,128)(2,1)S(1)}, u32[]{:S(2)}, u32[]{:S(2)}) async-start(bf16[1,48,64,128]{3,2,0,1:T(8,128)(2,1)} %bitcast.32), calls=%async_computation.5 | async-start | bytes 1572864 | tf_op jit(solution)/shard_map/all_to_all | solution.py:168
  168.5 1.7 gather_fusion
  170.3 1.8 gather_fusion.4
  172.1 34.8 %all-reduce.9 = (f32[128]{0:T(128)S(1)}, f32[128]{0:T(128)S(1)}) all-reduce(f32[128]{0:T(128)S(1)} %copy-done.50, f32[128]{0:T(128)S(1)} %copy-done.52), channel_id=1, replica_groups=mesh['seq'=16,'head'=16] {'seq'}, use_global_device_ids=true, to_apply=%region_4.5 | all-reduce | flops 256 | bytes 2048 | tf_op jit(solution)/shard_map/psum | solution.py:15
  209.9 2.5 collective-permute-start.5
  212.4 5.4 collective-permute-start.4
  217.8 1.9 collective-permute-start.6
  220.5 3.9 collective-permute-start.7
  224.5 8.8 %all-to-all-start.6 = ((bf16[1,48,64,128]{3,2,0,1:T(8,128)(2,1)}), bf16[1,48,64,128]{3,2,0,1:T(8,128)(2,1)}, u32[]{:S(2)}, u32[]{:S(2)}) async-start(bf16[1,48,64,128]{3,2,0,1:T(8,128)(2,1)} %bitcast.35), calls=%async_computation.6 | async-start | bytes 1572864 | tf_op jit(solution)/shard_map/all_to_all | solution.py:169
  233.3 83.0 %all-reduce.17.cloned.1.call-done = (bf16[128,128]{1,0:T(8,128)(2,1)}, bf16[128,128]{1,0:T(8,128)(2,1)}, bf16[128,128]{1,0:T(8,128)(2,1)}, bf16[128,128]{1,0:T(8,128)(2,1)}) async-done(((bf16[128,128]{1,0:T(8,128)(2,1)}, bf16[128,128]{1,0:T(8,128)(2,1)}, bf16[128,128]{1,0:T(8,128)(2,1)}, bf16[128,128]{1,0:T(8,128)(2,1)}), (bf16[128,128]{1,0:T(8,128)(2,1)}, bf16[128,128]{1,0:T(8,128)(2,1)}, ...) | async-done | bytes 131088 | tf_op jit(solution)/shard_map/psum | solution.py:15
  321.2 1.7 exponential_select_fusion
  322.9 2.3 multiply_convert_fusion
  325.2 1.6 multiply_bitcast_fusion
  326.8 14.7 %all-to-all-start.8 = ((f32[1,48,64,128]{3,2,0,1:T(8,128)}), f32[1,48,64,128]{3,2,0,1:T(8,128)}, u32[]{:S(2)}, u32[]{:S(2)}) async-start(f32[1,48,64,128]{3,2,0,1:T(8,128)} %multiply_bitcast_fusion), calls=%async_computation.8 | async-start | bytes 3145728 | tf_op jit(solution)/shard_map/all_to_all | solution.py:184
  341.8 1.8 fusion.49
  343.6 1.8 copy.139
  351.7 140.2 %all-reduce.15.cloned.1.call-done = (bf16[1,128,128]{2,1,0:T(8,128)(2,1)}, bf16[1,128,128]{2,1,0:T(8,128)(2,1)}, bf16[1,128,128]{2,1,0:T(8,128)(2,1)}) async-done(((bf16[1,128,128]{2,1,0:T(8,128)(2,1)}, bf16[1,128,128]{2,1,0:T(8,128)(2,1)}, bf16[1,128,128]{2,1,0:T(8,128)(2,1)}), (bf16[1,128,128]{2,1,0:T(8,128)(2,1)}, bf16[1,128,128]{2,1,0:T(8,128)(2,1)}, ...) | async-done | bytes 98320 | tf_op jit(solution)/shard_map/psum | solution.py:151
  495.1 3.0 convolution_bitcast_fusion
  498.1 10.7 %all-to-all-start.10 = ((f32[1,48,64,128]{3,2,0,1:T(8,128)}), f32[1,48,64,128]{3,2,0,1:T(8,128)}, u32[]{:S(2)}, u32[]{:S(2)}) async-start(f32[1,48,64,128]{3,2,0,1:T(8,128)} %convolution_bitcast_fusion), calls=%async_computation.10 | async-start | bytes 3145728 | tf_op jit(solution)/shard_map/all_to_all | solution.py:185
  508.9 1.5 convolution_multiply_fusion
  510.4 5.4 scatter_fusion
  517.1 2.2 reduce.25
  520.1 5.4 scatter_fusion.1
  532.5 4.7 all-to-all-done.10
  537.2 9.0 %all-to-all-start.7 = ((bf16[16,2,4096]{2,1,0:T(2,128)(2,1)}), bf16[16,2,4096]{2,1,0:T(2,128)(2,1)S(1)}, u32[]{:S(2)}, u32[]{:S(2)}) async-start(bf16[16,2,4096]{2,1,0:T(2,128)(2,1)} %reshape.1101), calls=%async_computation.7 | async-start | bytes 524288 | tf_op jit(solution)/shard_map/all_to_all | solution.py:235
  546.2 5.4 scatter_fusion.2
  554.1 2.2 reduce.26
  559.4 8.4 %all-to-all-start.11 = ((bf16[16,2,4096]{2,1,0:T(2,128)(2,1)}), bf16[16,2,4096]{2,1,0:T(2,128)(2,1)S(1)}, u32[]{:S(2)}, u32[]{:S(2)}) async-start(bf16[16,2,4096]{2,1,0:T(2,128)(2,1)} %reshape.1103), calls=%async_computation.11 | async-start | bytes 524288 | tf_op jit(solution)/shard_map/all_to_all | solution.py:237
  569.7 11.4 %all-to-all-done.11 = bf16[16,2,4096]{2,1,0:T(2,128)(2,1)S(1)} async-done(((bf16[16,2,4096]{2,1,0:T(2,128)(2,1)}), bf16[16,2,4096]{2,1,0:T(2,128)(2,1)S(1)}, u32[]{:S(2)}, u32[]{:S(2)}) %all-to-all-start.11) | async-done | bytes 262176 | tf_op jit(solution)/shard_map/all_to_all | solution.py:237
  581.1 3.5 all-to-all-start.9
  586.8 9.9 %all-to-all-done.9 = bf16[16,1,64,128]{3,2,1,0:T(8,128)(2,1)S(1)} async-done(((bf16[16,1,64,128]{3,2,1,0:T(8,128)(2,1)}), bf16[16,1,64,128]{3,2,1,0:T(8,128)(2,1)S(1)}, u32[]{:S(2)}, u32[]{:S(2)}) %all-to-all-start.9) | async-done | bytes 262176 | tf_op jit(solution)/shard_map/all_to_all | solution.py:232
  (318 shorter events, 95.9 us)
Async XLA Ops:
  8.9 53.7 %all-to-all-start = ((bf16[16,64,128]{2,1,0:T(8,128)(2,1)}), bf16[16,64,128]{2,1,0:T(8,128)(2,1)S(1)}, u32[]{:S(2)}, u32[]{:S(2)}) async-start(bf16[16,64,128]{2,1,0:T(8,128)(2,1)} %bitcast_bitcast_fusion.4), calls=%async_computation | async-start | bytes 524288 | tf_op jit(solution)/shard_map/all_to_all | solution.py:82
  51.5 5.6 copy-start.33
  51.5 9.8 %copy-start.32 = (f32[1,1024]{1,0:T(1,128)S(1)}, f32[1,1024]{1,0:T(1,128)}, u32[]{:S(2)}) copy-start(f32[1,1024]{1,0:T(1,128)} %param.30) | copy-start | bytes 12292
  51.5 10.3 %copy-start.25 = (bf16[64,2048]{1,0:T(8,128)(2,1)S(1)}, bf16[64,2048]{1,0:T(8,128)(2,1)}, u32[]{:S(2)}) copy-start(bf16[64,2048]{1,0:T(8,128)(2,1)} %param.27) | copy-start | bytes 786436
  51.5 21.9 %copy-start.26 = (bf16[64,2048]{1,0:T(8,128)(2,1)S(1)}, bf16[64,2048]{1,0:T(8,128)(2,1)}, u32[]{:S(2)}) copy-start(bf16[64,2048]{1,0:T(8,128)(2,1)} %param.28) | copy-start | bytes 786436
  56.8 34.3 %copy-start.27 = (bf16[64,2048]{1,0:T(8,128)(2,1)S(1)}, bf16[64,2048]{1,0:T(8,128)(2,1)}, u32[]{:S(2)}) copy-start(bf16[64,2048]{1,0:T(8,128)(2,1)} %param.25) | copy-start | bytes 786436
  56.9 35.1 %copy-start.28 = (bf16[64,2048]{1,0:T(8,128)(2,1)S(1)}, bf16[64,2048]{1,0:T(8,128)(2,1)}, u32[]{:S(2)}) copy-start(bf16[64,2048]{1,0:T(8,128)(2,1)} %param.29) | copy-start | bytes 786436
  60.5 62.4 %copy-start.39 = (s32[1024]{0:T(1024)}, s32[1024]{0:T(1024)S(1)}, u32[]{:S(2)}) copy-start(s32[1024]{0:T(1024)S(1)} %pad_clamp_fusion.1) | copy-start | bytes 12292
  60.7 32.0 %copy-start.40 = (s32[48]{0:T(128)}, s32[48]{0:T(128)S(1)}, u32[]{:S(2)}) copy-start(s32[48]{0:T(128)S(1)} %fusion.115) | copy-start | bytes 580
  62.6 24.4 %all-to-all-start.2 = ((bf16[16,64,128]{2,1,0:T(8,128)(2,1)}), bf16[16,64,128]{2,1,0:T(8,128)(2,1)S(1)}, u32[]{:S(2)}, u32[]{:S(2)}) async-start(bf16[16,64,128]{2,1,0:T(8,128)(2,1)} %bitcast_bitcast_fusion.2), calls=%async_computation.2 | async-start | bytes 524288 | tf_op jit(solution)/shard_map/all_to_all | solution.py:83
  87.0 16.4 %all-to-all-start.4 = ((bf16[16,64,128]{2,1,0:T(8,128)(2,1)}), bf16[16,64,128]{2,1,0:T(8,128)(2,1)S(1)}, u32[]{:S(2)}, u32[]{:S(2)}) async-start(bf16[16,64,128]{2,1,0:T(8,128)(2,1)} %bitcast_bitcast_fusion), calls=%async_computation.4 | async-start | bytes 524288 | tf_op jit(solution)/shard_map/all_to_all | solution.py:84
  103.4 15.6 %all-to-all-start.3 = ((bf16[16,64,128]{2,1,0:T(8,128)(2,1)}), bf16[16,64,128]{2,1,0:T(8,128)(2,1)S(1)}, u32[]{:S(2)}, u32[]{:S(2)}) async-start(bf16[16,64,128]{2,1,0:T(8,128)(2,1)} %bitcast_bitcast_fusion.1), calls=%async_computation.3 | async-start | bytes 524288 | tf_op jit(solution)/shard_map/all_to_all | solution.py:85
  119.0 15.5 %all-to-all-start.1 = ((bf16[16,64,128]{2,1,0:T(8,128)(2,1)}), bf16[16,64,128]{2,1,0:T(8,128)(2,1)S(1)}, u32[]{:S(2)}, u32[]{:S(2)}) async-start(bf16[16,64,128]{2,1,0:T(8,128)(2,1)} %bitcast_bitcast_fusion.3), calls=%async_computation.1 | async-start | bytes 524288 | tf_op jit(solution)/shard_map/all_to_all | solution.py:81
  135.7 71.3 %collective-permute-start.2 = (bf16[1,1,64,128]{3,2,1,0:T(8,128)(2,1)}, bf16[1,1,64,128]{3,2,1,0:T(8,128)(2,1)S(1)}, u32[]{:S(2)}, u32[]{:S(2)}) collective-permute-start(bf16[1,1,64,128]{3,2,1,0:T(8,128)(2,1)} %get-tuple-element.144), channel_id=1, source_target_pairs={{16,0},{32,16},{48,32},{64,48},{80,64},{96,80},{112,96},{128,112},... | collective-permute-start | bytes 49160 | tf_op jit(solution)/shard_map/ppermute | solution.py:21
  141.1 65.8 %collective-permute-start = (bf16[1,1,64,128]{3,2,1,0:T(8,128)(2,1)}, bf16[1,1,64,128]{3,2,1,0:T(8,128)(2,1)S(1)}, u32[]{:S(2)}, u32[]{:S(2)}) collective-permute-start(bf16[1,1,64,128]{3,2,1,0:T(8,128)(2,1)} %get-tuple-element.145), channel_id=1, source_target_pairs={{0,16},{16,32},{32,48},{48,64},{64,80},{80,96},{96,112},{112,128},... | collective-permute-start | bytes 49160 | tf_op jit(solution)/shard_map/ppermute | solution.py:21
  143.7 65.3 %collective-permute-start.3 = (bf16[1,1,64,128]{3,2,1,0:T(8,128)(2,1)S(1)}, bf16[1,1,64,128]{3,2,1,0:T(8,128)(2,1)S(1)}, u32[]{:S(2)}, u32[]{:S(2)}) collective-permute-start(bf16[1,1,64,128]{3,2,1,0:T(8,128)(2,1)S(1)} %get-tuple-element.142), channel_id=1, source_target_pairs={{16,0},{32,16},{48,32},{64,48},{80,64},{96,80},{112,96},{128,112},... | collective-permute-start | bytes 49160 | tf_op jit(solution)/shard_map/ppermute | solution.py:21
  149.7 58.3 %collective-permute-start.1 = (bf16[1,1,64,128]{3,2,1,0:T(8,128)(2,1)S(1)}, bf16[1,1,64,128]{3,2,1,0:T(8,128)(2,1)S(1)}, u32[]{:S(2)}, u32[]{:S(2)}) collective-permute-start(bf16[1,1,64,128]{3,2,1,0:T(8,128)(2,1)S(1)} %get-tuple-element.143), channel_id=1, source_target_pairs={{0,16},{16,32},{32,48},{48,64},{64,80},{80,96},{96,112},{112,128},... | collective-permute-start | bytes 49160 | tf_op jit(solution)/shard_map/ppermute | solution.py:21
  155.8 68.7 %all-to-all-start.5 = ((bf16[1,48,64,128]{3,2,0,1:T(8,128)(2,1)}), bf16[1,48,64,128]{3,2,0,1:T(8,128)(2,1)S(1)}, u32[]{:S(2)}, u32[]{:S(2)}) async-start(bf16[1,48,64,128]{3,2,0,1:T(8,128)(2,1)} %bitcast.32), calls=%async_computation.5 | async-start | bytes 1572864 | tf_op jit(solution)/shard_map/all_to_all | solution.py:168
  163.1 153.2 %all-reduce.17.cloned.1.call-start = ((), (), s32[]{:S(2)}) async-start(), calls=%async_computation.13 | async-start | bytes 262144 | tf_op jit(solution)/shard_map/psum | solution.py:15
  163.4 3.4 copy-start.18
  168.5 3.6 copy-start.50
  168.5 3.6 copy-start.52
  168.5 38.4 %copy-start.49 = (f32[64]{0:T(128)S(1)}, f32[64]{0:T(128)}, u32[]{:S(2)}) copy-start(f32[64]{0:T(128)} %get-tuple-element.153) | copy-start | bytes 772
  168.5 38.6 %copy-start.48 = (f32[64]{0:T(128)S(1)}, f32[64]{0:T(128)}, u32[]{:S(2)}) copy-start(f32[64]{0:T(128)} %get-tuple-element.152) | copy-start | bytes 772
  168.5 39.5 %copy-start.46 = (f32[64]{0:T(128)S(1)}, f32[64]{0:T(128)}, u32[]{:S(2)}) copy-start(f32[64]{0:T(128)} %get-tuple-element.151) | copy-start | bytes 772
  168.5 40.4 %copy-start.45 = (f32[64]{0:T(128)S(1)}, f32[64]{0:T(128)}, u32[]{:S(2)}) copy-start(f32[64]{0:T(128)} %get-tuple-element.150) | copy-start | bytes 772
  170.3 146.1 %copy-start.42 = (pred[1024]{0:T(1024)(128)(4,1)S(1)}, pred[1024]{0:T(1024)(128)(4,1)}, u32[]{:S(2)}) copy-start(pred[1024]{0:T(1024)(128)(4,1)} %broadcast_in_dim.110) | copy-start | bytes 3076
  206.9 110.4 %copy-start.37 = (bf16[1,1,64,128]{3,2,1,0:T(8,128)(2,1)}, bf16[1,1,64,128]{3,2,1,0:T(8,128)(2,1)S(1)}, u32[]{:S(2)}) copy-start(bf16[1,1,64,128]{3,2,1,0:T(8,128)(2,1)S(1)} %collective-permute-done) | copy-start | bytes 49156
  207.1 26.2 %copy-start.35 = (bf16[1,1,64,128]{3,2,1,0:T(8,128)(2,1)}, bf16[1,1,64,128]{3,2,1,0:T(8,128)(2,1)S(1)}, u32[]{:S(2)}) copy-start(bf16[1,1,64,128]{3,2,1,0:T(8,128)(2,1)S(1)} %collective-permute-done.2) | copy-start | bytes 49156
  209.9 316.4 %collective-permute-start.5 = (bf16[1,1,64,128]{3,2,1,0:T(8,128)(2,1)}, bf16[1,1,64,128]{3,2,1,0:T(8,128)(2,1)}, u32[]{:S(2)}, u32[]{:S(2)}) collective-permute-start(bf16[1,1,64,128]{3,2,1,0:T(8,128)(2,1)} %fusion.58), channel_id=1, source_target_pairs={{0,16},{16,32},{32,48},{48,64},{64,80},{80,96},{96,112},{112,128},... | collective-permute-start | bytes 49160 | tf_op jit(solution)/shard_map/ppermute | solution.py:21
  212.4 313.1 %collective-permute-start.4 = (bf16[1,1,64,128]{3,2,1,0:T(8,128)(2,1)}, bf16[1,1,64,128]{3,2,1,0:T(8,128)(2,1)}, u32[]{:S(2)}, u32[]{:S(2)}) collective-permute-start(bf16[1,1,64,128]{3,2,1,0:T(8,128)(2,1)} %fusion.59), channel_id=1, source_target_pairs={{16,0},{32,16},{48,32},{64,48},{80,64},{96,80},{112,96},{128,112},... | collective-permute-start | bytes 49160 | tf_op jit(solution)/shard_map/ppermute | solution.py:21
  217.8 333.8 %collective-permute-start.6 = (bf16[1,1,64,128]{3,2,1,0:T(8,128)(2,1)}, bf16[1,1,64,128]{3,2,1,0:T(8,128)(2,1)}, u32[]{:S(2)}, u32[]{:S(2)}) collective-permute-start(bf16[1,1,64,128]{3,2,1,0:T(8,128)(2,1)} %fusion.56), channel_id=1, source_target_pairs={{16,0},{32,16},{48,32},{64,48},{80,64},{96,80},{112,96},{128,112},... | collective-permute-start | bytes 49160 | tf_op jit(solution)/shard_map/ppermute | solution.py:21
  220.5 332.4 %collective-permute-start.7 = (bf16[1,1,64,128]{3,2,1,0:T(8,128)(2,1)}, bf16[1,1,64,128]{3,2,1,0:T(8,128)(2,1)S(1)}, u32[]{:S(2)}, u32[]{:S(2)}) collective-permute-start(bf16[1,1,64,128]{3,2,1,0:T(8,128)(2,1)} %fusion.57), channel_id=1, source_target_pairs={{0,16},{16,32},{32,48},{48,64},{64,80},{80,96},{96,112},{112,128},... | collective-permute-start | bytes 49160 | tf_op jit(solution)/shard_map/ppermute | solution.py:21
  224.5 91.8 %copy-start.1 = (bf16[1,48,64,128]{3,2,0,1:T(8,128)(2,1)}, bf16[1,48,64,128]{3,2,0,1:T(8,128)(2,1)S(1)}, u32[]{:S(2)}) copy-start(bf16[1,48,64,128]{3,2,0,1:T(8,128)(2,1)S(1)} %all-to-all-done.5) | copy-start | bytes 2359300
  224.5 98.4 %all-to-all-start.6 = ((bf16[1,48,64,128]{3,2,0,1:T(8,128)(2,1)}), bf16[1,48,64,128]{3,2,0,1:T(8,128)(2,1)}, u32[]{:S(2)}, u32[]{:S(2)}) async-start(bf16[1,48,64,128]{3,2,0,1:T(8,128)(2,1)} %bitcast.35), calls=%async_computation.6 | async-start | bytes 1572864 | tf_op jit(solution)/shard_map/all_to_all | solution.py:169
  326.8 171.3 %all-to-all-start.8 = ((f32[1,48,64,128]{3,2,0,1:T(8,128)}), f32[1,48,64,128]{3,2,0,1:T(8,128)}, u32[]{:S(2)}, u32[]{:S(2)}) async-start(f32[1,48,64,128]{3,2,0,1:T(8,128)} %multiply_bitcast_fusion), calls=%async_computation.8 | async-start | bytes 3145728 | tf_op jit(solution)/shard_map/all_to_all | solution.py:184
  341.5 6.0 copy-start.11
  341.5 6.0 copy-start.30
  341.5 150.3 %all-reduce.15.cloned.1.call-start = ((), (), s32[]{:S(2)}) async-start(), calls=%async_computation.12 | async-start | bytes 196608 | tf_op jit(solution)/shard_map/psum | solution.py:151
  343.6 4.2 copy-start.12
  498.1 10.8 %copy-start.3 = (bf16[1,48,64,128]{3,2,0,1:T(8,128)(2,1)S(1)}, bf16[1,48,64,128]{3,2,0,1:T(8,128)(2,1)}, u32[]{:S(2)}) copy-start(bf16[1,48,64,128]{3,2,0,1:T(8,128)(2,1)} %copy-done.1) | copy-start | bytes 2359300
  498.1 39.0 %all-to-all-start.10 = ((f32[1,48,64,128]{3,2,0,1:T(8,128)}), f32[1,48,64,128]{3,2,0,1:T(8,128)}, u32[]{:S(2)}, u32[]{:S(2)}) async-start(f32[1,48,64,128]{3,2,0,1:T(8,128)} %convolution_bitcast_fusion), calls=%async_computation.10 | async-start | bytes 3145728 | tf_op jit(solution)/shard_map/all_to_all | solution.py:185
  510.4 5.4 copy-start.38
  510.4 5.6 copy-start.36
  515.9 4.2 copy-start.41
  537.2 22.3 %all-to-all-start.7 = ((bf16[16,2,4096]{2,1,0:T(2,128)(2,1)}), bf16[16,2,4096]{2,1,0:T(2,128)(2,1)S(1)}, u32[]{:S(2)}, u32[]{:S(2)}) async-start(bf16[16,2,4096]{2,1,0:T(2,128)(2,1)} %reshape.1101), calls=%async_computation.7 | async-start | bytes 524288 | tf_op jit(solution)/shard_map/all_to_all | solution.py:235
  559.4 21.7 %all-to-all-start.11 = ((bf16[16,2,4096]{2,1,0:T(2,128)(2,1)}), bf16[16,2,4096]{2,1,0:T(2,128)(2,1)S(1)}, u32[]{:S(2)}, u32[]{:S(2)}) async-start(bf16[16,2,4096]{2,1,0:T(2,128)(2,1)} %reshape.1103), calls=%async_computation.11 | async-start | bytes 524288 | tf_op jit(solution)/shard_map/all_to_all | solution.py:237
  581.1 15.6 %all-to-all-start.9 = ((bf16[16,1,64,128]{3,2,1,0:T(8,128)(2,1)}), bf16[16,1,64,128]{3,2,1,0:T(8,128)(2,1)S(1)}, u32[]{:S(2)}, u32[]{:S(2)}) async-start(bf16[16,1,64,128]{3,2,1,0:T(8,128)(2,1)} %constant_dynamic-update-slice_fusion), calls=%async_computation.9 | async-start | bytes 524288 | tf_op jit(solution)/shard_map/all_to_all | solution.py:232
  (32 other events, 51.0 us)
Sparse Core Ops, SparseCore 0:
  167.8 148.4 all-reduce.16
  346.4 145.4 all-reduce.14
